TPU v7x, 128 devices: a whole 4x4x4 slice. The times are simulated.
128 devices in a mesh: pool: 8 (over x, core), wide: 8 (over y, z_hi), narrow: 2 (over z_lo).
Axes of the slice: x: 4, y: 4, z: 4 (z_hi: 2, z_lo: 2; z = z_hi * 2 + z_lo), core: 2. Of those that a mesh axis runs over, the one named last changes fastest.
Arguments:
- states: bfloat16 [384, 2560], P('pool'), may hold values from -3 to 3
- gain_in: float32 [2560], replicated, may hold values from 0.1 to 1.9
- w_qkv: bfloat16 [2560, 8, 6, 128], P('narrow', 'wide'), may hold values from -0.125 to 0.125
- q_gain: float32 [128], replicated, may hold values from 0.1 to 1.9
- k_gain: float32 [128], replicated, may hold values from 0.1 to 1.9
- key_cache: bfloat16 [2304, 8, 128, 128], P('pool', 'wide', 'narrow'), as said below
- value_cache: bfloat16 [2304, 8, 128, 128], P('pool', 'wide', 'narrow'), may hold values from -12 to 12
- cache_len: int32 [384], replicated, may hold values from 1 to 8192, as said below
- page_table: int32 [384, 64], replicated, may hold values from -1 to 2303, as said below
- w_out: bfloat16 [4096, 2560], P('wide'), may hold values from -0.125 to 0.125
- gain_post: float32 [2560], replicated, may hold values from 0.1 to 1.9
- w_gate_up: bfloat16 [2560, 2, 9728], P(None, None, ('wide', 'narrow')), may hold values from -0.125 to 0.125
- w_down: bfloat16 [9728, 2560], P(('wide', 'narrow')), may hold values from -0.078125 to 0.078125
Outputs:
- attn_mixed: bfloat16 [384, 2560], P('pool')
- layer_out: bfloat16 [384, 2560], P('pool')
Inputs may be any that keep to these rules, and one draw needn't show every extreme that they name: `cache_len`: exactly one request has 8192 cached tokens; every other request has at most (5) * 128. `page_table`: entry (r, b) is pool device times 288 plus slot of the page with tokens b * 128 to (b + 1) * 128 - 1 of request r for b < ceil(cache_len[r] / 128), and -1 for later b; no slot is named twice. One pool device holds exactly 288 pages; the others hold the remaining pages, within one page of each other. `key_cache`: cached keys.
All inputs are finite; a program needn't handle non-finite values.
Results may differ from a plain program's by a relative error of at most 0.012.
The roundings to bfloat16 on the way count: a program that leaves them out, or rounds other values in their place, can miss the bound.
Values may be sent and summed in bfloat16 or wider, within the bound.
No kernel may reach another device: no remote copies, remote signals or barrier semaphores. Data moves between devices by JAX's collectives and lax.ppermute only.
A program may use at most 128 MiB of HBM per device.

v0:
```python
import math
import jax
import jax.numpy as jnp
from jax import lax
from jax.sharding import PartitionSpec as P

epsilon = 1e-06
rope_base = 1000000.0
masked_score = -1e30


def rms_scale(values, gain):
    return values * lax.rsqrt(jnp.mean(values * values, axis=-1, keepdims=True) + epsilon) * gain


def rotate(values, angle_pos):
    half = values.shape[-1] // 2
    ramp = jnp.arange(half).astype(jnp.float32)
    freqs = jnp.exp(ramp * (-2.0 * math.log(rope_base) / values.shape[-1]))
    angle = angle_pos[..., None] * freqs
    cosine = jnp.cos(angle)
    sine = jnp.sin(angle)
    lower = values[..., :half]
    upper = values[..., half:]
    return jnp.concatenate([lower * cosine - upper * sine, upper * cosine + lower * sine], axis=-1)


def feed_forward(normed_post, w_gate_up):
    gate_up = jnp.einsum("rd,dcf->rcf", normed_post, w_gate_up, preferred_element_type=jnp.float32)
    return (jax.nn.silu(gate_up[:, 0]) * gate_up[:, 1]).astype(jnp.bfloat16)


def per_device(
    states,
    gain_in,
    w_qkv,
    q_gain,
    k_gain,
    key_cache,
    value_cache,
    cache_len,
    page_table,
    w_out,
    gain_post,
    w_gate_up,
    w_down,
):
    kv_local = w_qkv.shape[1]
    group = w_qkv.shape[2] - 2
    head_dim = w_qkv.shape[3]
    scale = head_dim ** (-0.5)
    narrow_size = lax.axis_size("narrow")
    narrow_index = lax.axis_index("narrow")
    pool_index = lax.axis_index("pool")
    resid_in = states.astype(jnp.float32)
    normed = rms_scale(resid_in, gain_in).astype(jnp.bfloat16)
    part_width = w_qkv.shape[0]
    own_part = lax.dynamic_slice_in_dim(normed, narrow_index * part_width, part_width, 1)
    partial_proj = jnp.einsum("rd,dkch->rkch", own_part, w_qkv, preferred_element_type=jnp.float32)
    proj = lax.psum_scatter(partial_proj, "narrow", scatter_dimension=0, tiled=True)
    row_count = proj.shape[0]
    first_row = (pool_index * narrow_size + narrow_index) * row_count
    own_len = lax.dynamic_slice_in_dim(cache_len, first_row, row_count, 0)
    position = own_len.astype(jnp.float32)
    query = rotate(
        rms_scale(proj[:, :, :group], q_gain),
        jnp.broadcast_to(position[:, None, None], (row_count, kv_local, group)),
    ).astype(jnp.bfloat16)
    key_new = rotate(rms_scale(proj[:, :, group], k_gain), position[:, None]).astype(jnp.bfloat16)
    value_new = proj[:, :, group + 1].astype(jnp.bfloat16)
    all_queries = lax.all_gather(query, ("pool", "narrow"), axis=0, tiled=True)
    slot_count = key_cache.shape[0]
    half_page = key_cache.shape[2]
    holder_count = lax.axis_size("pool")
    req_count = page_table.shape[0]
    max_blocks = page_table.shape[1]
    flat_pages = page_table.reshape(-1)
    entry = jnp.arange(req_count * max_blocks, dtype=jnp.int32)
    target = jnp.where(flat_pages >= 0, flat_pages, holder_count * slot_count)
    owner_all = (
        jnp.full((holder_count * slot_count,), -1, jnp.int32)
        .at[target]
        .set(entry // max_blocks, mode="drop")
    )
    block_all = (
        jnp.zeros((holder_count * slot_count,), jnp.int32)
        .at[target]
        .set(entry % max_blocks, mode="drop")
    )
    owner = lax.dynamic_slice_in_dim(owner_all, pool_index * slot_count, slot_count, 0)
    block = lax.dynamic_slice_in_dim(block_all, pool_index * slot_count, slot_count, 0)
    safe_owner = jnp.maximum(owner, 0)
    page_len = half_page * narrow_size
    token_pos = (
        block[:, None] * page_len
        + narrow_index * half_page
        + jnp.arange(half_page, dtype=jnp.int32)[None, :]
    )
    live = (owner[:, None] >= 0) & (token_pos < cache_len[safe_owner][:, None])
    live_mask = live[:, None, None, :]
    slot_query = all_queries[safe_owner]
    scores = (
        jnp.einsum("skgd,sktd->skgt", slot_query, key_cache, preferred_element_type=jnp.float32)
        * scale
    )
    slot_top = jnp.max(jnp.where(live_mask, scores, masked_score), axis=-1)
    member = owner[:, None] == jnp.arange(req_count, dtype=jnp.int32)[None, :]
    req_top = jnp.max(jnp.where(member[:, :, None, None], slot_top[:, None], masked_score), axis=0)
    expo = jnp.where(live_mask, jnp.exp(scores - req_top[safe_owner][..., None]), 0.0)
    slot_total = jnp.sum(expo, axis=-1)
    slot_out = jnp.einsum(
        "skgt,sktd->skgd",
        expo.astype(jnp.bfloat16),
        value_cache,
        preferred_element_type=jnp.float32,
    )
    member_weight = member.astype(jnp.float32)
    req_out = jnp.einsum(
        "sr,sx->rx",
        member_weight,
        slot_out.reshape(slot_count, -1),
        precision=lax.Precision.HIGHEST,
    )
    req_out = req_out.reshape(req_count, kv_local, group, head_dim)
    req_total = jnp.einsum(
        "sr,sx->rx",
        member_weight,
        slot_total.reshape(slot_count, -1),
        precision=lax.Precision.HIGHEST,
    )
    req_total = req_total.reshape(req_count, kv_local, group)
    got_out, got_top, got_total = (
        lax.all_to_all(req_out[None], ("pool", "narrow"), split_axis=1, concat_axis=0, tiled=True),
        lax.all_to_all(req_top[None], ("pool", "narrow"), split_axis=1, concat_axis=0, tiled=True),
        lax.all_to_all(
            req_total[None], ("pool", "narrow"), split_axis=1, concat_axis=0, tiled=True
        ),
    )
    own_score = (
        jnp.einsum("rkgd,rkd->rkg", query, key_new, preferred_element_type=jnp.float32) * scale
    )
    top = jnp.maximum(jnp.max(got_top, axis=0), own_score)
    factor = jnp.exp(got_top - top[None])
    own_expo = jnp.exp(own_score - top)
    total = jnp.sum(got_total * factor, axis=0) + own_expo
    own_term = jnp.einsum(
        "rkg,rkd->rkgd",
        own_expo.astype(jnp.bfloat16),
        value_new,
        preferred_element_type=jnp.float32,
    )
    summed = jnp.sum(got_out * factor[..., None], axis=0) + own_term
    attn = (
        (summed / total[..., None])
        .astype(jnp.bfloat16)
        .reshape(row_count, kv_local * group * head_dim)
    )
    partial_out = jnp.dot(
        lax.all_gather(attn, "narrow", axis=0, tiled=True),
        w_out,
        preferred_element_type=jnp.float32,
    )
    mixed = lax.psum(partial_out, "wide")
    resid = resid_in + mixed
    attn_mixed = mixed.astype(jnp.bfloat16)
    normed_post = rms_scale(resid, gain_post).astype(jnp.bfloat16)
    hidden = feed_forward(normed_post, w_gate_up)
    down = jnp.dot(hidden, w_down, preferred_element_type=jnp.float32)
    layer_out = (resid + lax.psum(down, ("wide", "narrow"))).astype(jnp.bfloat16)
    return (attn_mixed, layer_out)


def solution(mesh):
    in_specs = (
        P("pool", None),
        P(),
        P("narrow", "wide", None, None),
        P(),
        P(),
        P("pool", "wide", "narrow", None),
        P("pool", "wide", "narrow", None),
        P(),
        P(),
        P("wide", None),
        P(),
        P(None, None, ("wide", "narrow")),
        P(("wide", "narrow"), None),
    )
    out_specs = (P("pool", None), P("pool", None))
    return jax.shard_map(
        per_device, mesh=mesh, in_specs=in_specs, out_specs=out_specs, check_vma=False
    )
```

profile of v0, /device:TPU:0, one launch (start us, length us, event | category | flops | bytes accessed | tf_op | source)
XLA Modules:
  0.0 489.5 jit_solution(1775987561983351854)
XLA Ops:
  7.2 1.2 multiply_reduce_fusion.1
  8.5 1.8 convert_element_type.67
  10.3 0.8 dynamic-slice
  11.0 2.9 fusion.9
  14.0 0.7 fusion.32
  15.1 90.5 %scatter_custom_fusion.1 = s32[2304]{0:T(1024)S(1)} fusion(s32[24576]{0:T(1024)S(1)} %bitcast.105, s32[24576]{0:T(1024)} %fusion.32, s32[]{:T(128)} %constant.29.clone.1), kind=kCustom, calls=%fused_computation.110 | custom fusion | bytes 9728 | tf_op jit(solution)/shard_map/scatter | solution.py:88
  105.6 90.2 %scatter_custom_fusion = s32[2304]{0:T(1024)S(1)} fusion(s32[24576]{0:T(1024)S(1)} %bitcast.106, s32[24576]{0:T(1024)S(1)} %add_select_fusion, s32[]{:T(128)} %constant.28.clone.1), kind=kCustom, calls=%fused_computation.112 | custom fusion | bytes 9220 | tf_op jit(solution)/shard_map/scatter | solution.py:83
  196.0 2.4 gather_fusion
  198.7 0.8 iota_compare_fusion
  199.5 0.8 multiply_reduce_fusion.4
  200.3 0.9 multiply_reduce_fusion.3
  201.2 0.8 multiply_multiply_fusion.1
  202.0 0.7 fusion.76
  202.8 0.9 multiply_multiply_fusion
  203.9 32.0 %all_gather.6 = bf16[384,1,4,128]{3,0,2,1:T(8,128)(2,1)S(1)} all-gather(bf16[24,1,4,128]{3,0,2,1:T(8,128)(2,1)S(1)} %pad_maximum_fusion), channel_id=1, replica_groups=mesh['pool'=8,'wide'=8,'narrow'=2] {'pool','narrow'}, dimensions={0}, use_global_device_ids=true | all-gather | bytes 417792 | tf_op jit(solution)/shard_map/all_gather | solution.py:71
  236.2 2.4 gather_fusion.1
  238.6 5.8 %select_reduce_fusion.1 = (f32[288,4]{1,0:T(8,128)S(1)}, f32[288,4,64]{2,1,0:T(4,128)}) fusion(pred[288,64]{1,0:T(8,128)(4,1)S(1)} %fusion.36, bf16[288,4,128]{2,1,0:T(4,128)(2,1)} %gather_fusion.1, bf16[288,1,64,128]{3,2,1,0:T(8,128)(2,1)} %param.18), kind=kOutput, calls=%fused_computation.23 | convolution fusion | flops 19094400 | bytes 5331456 | tf_op jit(solution)/shard_map/skgd,sktd->skgt/dot_general | solution.py:103
  245.0 0.8 copy.68
  245.8 3.5 all-to-all-start.1
  249.3 1.7 gather_fusion.2
  251.1 1.9 fusion.16
  253.0 4.8 fusion
  257.9 1.4 fusion.29
  259.5 0.8 fusion.58
  260.2 1.3 fusion.70
  261.5 5.6 %all-to-all-start.2 = ((f32[1,384,1,4]{3,2,0,1:T(1,128)}), f32[1,384,1,4]{3,2,0,1:T(1,128)S(1)}, u32[]{:S(2)}, u32[]{:S(2)}) async-start(f32[1,384,1,4]{3,2,0,1:T(1,128)} %bitcast.101), calls=%async_computation.3 | async-start | bytes 393216 | tf_op jit(solution)/shard_map/all_to_all | solution.py:135
  267.2 2.0 convolution_bitcast_fusion
  269.1 1.4 copy.67
  270.5 0.6 reduce_max.32
  271.2 3.5 all-to-all-done.2
  274.7 0.7 copy-done.3
  275.4 4.3 all-to-all-start
  279.7 0.8 multiply_maximum_fusion
  281.1 0.7 subtract_exponential_fusion
  281.8 1.7 copy.69
  283.5 1.0 multiply_reduce_fusion.2
  284.5 0.7 convert_convert_fusion
  285.4 8.9 %all-to-all-done = f32[1,384,1,4,128]{4,3,2,0,1:T(4,128)} async-done(((f32[1,384,1,4,128]{4,3,2,0,1:T(4,128)}), f32[1,384,1,4,128]{4,3,2,0,1:T(4,128)}, u32[]{:S(2)}, u32[]{:S(2)}) %all-to-all-start) | async-done | bytes 786464 | tf_op jit(solution)/shard_map/all_to_all | solution.py:133
  294.3 1.4 fusion.12
  295.7 0.8 copy_bitcast_fusion
  296.5 4.5 all_gather.7
  301.0 3.1 fusion.81
  304.2 85.7 %all-reduce.3.cloned.1.call-done = f32[48,2560]{1,0:T(8,128)} async-done(((f32[48,2560]{1,0:T(8,128)}), f32[48,2560]{1,0:T(8,128)}) %all-reduce.3.cloned.1.call-update) | async-done | bytes 491536 | tf_op jit(solution)/shard_map/psum | solution.py:163
  389.9 1.2 multiply_reduce_fusion
  391.1 4.9 fusion.23
  396.1 1.4 fusion.50
  397.5 83.2 %all-reduce.5.cloned.1.call-done = f32[48,2560]{1,0:T(8,128)} async-done(((f32[48,2560]{1,0:T(8,128)}), f32[48,2560]{1,0:T(8,128)}) %all-reduce.5.cloned.1.call-update) | async-done | bytes 491536 | tf_op jit(solution)/shard_map/psum | solution.py:169
  480.8 2.2 add_convert_fusion
  (70 shorter events, 3.1 us)
Async XLA Ops:
  7.2 388.9 %copy-start = (bf16[608,2560]{1,0:T(8,128)(2,1)S(1)}, bf16[608,2560]{1,0:T(8,128)(2,1)}, u32[]{:S(2)}) copy-start(bf16[608,2560]{1,0:T(8,128)(2,1)} %param.25) | copy-start | bytes 9338884
  7.2 7.4 %copy-start.11 = (s32[384,64]{0,1:T(8,128)S(1)}, s32[384,64]{0,1:T(8,128)}, u32[]{:S(2)}) copy-start(s32[384,64]{0,1:T(8,128)} %param.21) | copy-start | bytes 294916
  7.2 188.8 %copy-start.1 = (s32[384]{0:T(512)S(1)}, s32[384]{0:T(512)}, u32[]{:S(2)}) copy-start(s32[384]{0:T(512)} %param.20) | copy-start | bytes 4612
  7.2 192.3 %reduce-scatter.2.cloned.1.call-start = ((), (), s32[]{:S(2)}) async-start(), calls=%async_computation.4 | async-start | bytes 221184 | tf_op jit(solution)/shard_map/reduce_scatter | solution.py:60
  10.3 192.5 %copy-start.18 = (f32[128]{0:T(128)S(1)}, f32[128]{0:T(128)}, u32[]{:S(2)}) copy-start(f32[128]{0:T(128)} %param.16) | copy-start | bytes 1540
  195.9 40.0 %copy-start.12 = (s32[288]{0:T(512)}, s32[288]{0:T(512)S(1)}, u32[]{:S(2)}) copy-start(s32[288]{0:T(512)S(1)} %get-tuple-element.3) | copy-start | bytes 3460
  195.9 48.5 %copy-start.14 = (s32[1024]{0:T(1024)}, s32[1024]{0:T(1024)S(1)}, u32[]{:S(2)}) copy-start(s32[1024]{0:T(1024)S(1)} %pad_clamp_fusion) | copy-start | bytes 12292
  198.6 45.8 %copy-start.5 = (pred[288,64]{1,0:T(8,128)(4,1)}, pred[288,64]{1,0:T(8,128)(4,1)S(1)}, u32[]{:S(2)}) copy-start(pred[288,64]{1,0:T(8,128)(4,1)S(1)} %fusion.36) | copy-start | bytes 55300
  203.8 32.1 %copy-start.6 = (bf16[24,1,4,64]{3,0,2,1:T(8,128)(2,1)}, bf16[24,1,4,64]{3,0,2,1:T(8,128)(2,1)S(1)}, u32[]{:S(2)}) copy-start(bf16[24,1,4,64]{3,0,2,1:T(8,128)(2,1)S(1)} %get-tuple-element.6) | copy-start | bytes 36868
  203.8 32.1 %copy-start.8 = (bf16[24,1,4,64]{3,0,2,1:T(8,128)(2,1)}, bf16[24,1,4,64]{3,0,2,1:T(8,128)(2,1)S(1)}, u32[]{:S(2)}) copy-start(bf16[24,1,4,64]{3,0,2,1:T(8,128)(2,1)S(1)} %get-tuple-element.7) | copy-start | bytes 36868
  238.6 5.9 %copy-start.4 = (pred[288,384]{1,0:T(8,128)(4,1)S(1)}, pred[288,384]{1,0:T(8,128)(4,1)}, u32[]{:S(2)}) copy-start(pred[288,384]{1,0:T(8,128)(4,1)} %iota_compare_fusion) | copy-start | bytes 331780
  245.8 15.7 %all-to-all-start.1 = ((f32[1,384,1,4]{3,2,0,1:T(1,128)}), f32[1,384,1,4]{3,2,0,1:T(1,128)S(1)}, u32[]{:S(2)}, u32[]{:S(2)}) async-start(f32[1,384,1,4]{3,2,0,1:T(1,128)} %copy.68), calls=%async_computation.2 | async-start | bytes 393216 | tf_op jit(solution)/shard_map/all_to_all | solution.py:134
  252.9 4.9 %copy-start.13 = (s32[288]{0:T(512)S(1)}, s32[288]{0:T(512)}, u32[]{:S(2)}) copy-start(s32[288]{0:T(512)} %copy-done.12) | copy-start | bytes 3460
  253.0 6.3 %copy-start.15 = (bf16[24,64]{1,0:T(8,128)(2,1)S(1)}, bf16[24,64]{1,0:T(8,128)(2,1)}, u32[]{:S(2)}) copy-start(bf16[24,64]{1,0:T(8,128)(2,1)} %get-tuple-element.10) | copy-start | bytes 9220
  253.0 6.3 %copy-start.16 = (bf16[24,64]{1,0:T(8,128)(2,1)S(1)}, bf16[24,64]{1,0:T(8,128)(2,1)}, u32[]{:S(2)}) copy-start(bf16[24,64]{1,0:T(8,128)(2,1)} %get-tuple-element.11) | copy-start | bytes 9220
  253.0 6.4 %copy-start.7 = (bf16[24,1,4,64]{3,0,2,1:T(8,128)(2,1)S(1)}, bf16[24,1,4,64]{3,0,2,1:T(8,128)(2,1)}, u32[]{:S(2)}) copy-start(bf16[24,1,4,64]{3,0,2,1:T(8,128)(2,1)} %copy-done.6) | copy-start | bytes 36868
  253.0 6.4 %copy-start.9 = (bf16[24,1,4,64]{3,0,2,1:T(8,128)(2,1)S(1)}, bf16[24,1,4,64]{3,0,2,1:T(8,128)(2,1)}, u32[]{:S(2)}) copy-start(bf16[24,1,4,64]{3,0,2,1:T(8,128)(2,1)} %copy-done.8) | copy-start | bytes 36868
  261.5 13.2 %all-to-all-start.2 = ((f32[1,384,1,4]{3,2,0,1:T(1,128)}), f32[1,384,1,4]{3,2,0,1:T(1,128)S(1)}, u32[]{:S(2)}, u32[]{:S(2)}) async-start(f32[1,384,1,4]{3,2,0,1:T(1,128)} %bitcast.101), calls=%async_computation.3 | async-start | bytes 393216 | tf_op jit(solution)/shard_map/all_to_all | solution.py:135
  274.7 0.7 copy-start.3
  275.4 19.0 %all-to-all-start = ((f32[1,384,1,4,128]{4,3,2,0,1:T(4,128)}), f32[1,384,1,4,128]{4,3,2,0,1:T(4,128)}, u32[]{:S(2)}, u32[]{:S(2)}) async-start(f32[1,384,1,4,128]{4,3,2,0,1:T(4,128)} %copy.67), calls=%async_computation.1 | async-start | bytes 1572864 | tf_op jit(solution)/shard_map/all_to_all | solution.py:133
  279.6 110.3 %copy-start.2 = (bf16[48,2560]{1,0:T(8,128)(2,1)S(1)}, bf16[48,2560]{1,0:T(8,128)(2,1)}, u32[]{:S(2)}) copy-start(bf16[48,2560]{1,0:T(8,128)(2,1)} %param.13) | copy-start | bytes 737284
  279.7 110.3 %all-reduce.3.cloned.1.call-start = ((), (), s32[]{:S(2)}) async-start(), calls=%async_computation.5 | async-start | bytes 983040 | tf_op jit(solution)/shard_map/psum | solution.py:163
  280.5 0.6 copy-start.10
  284.5 106.7 %copy-start.17 = (f32[2560]{0:T(1024)S(1)}, f32[2560]{0:T(1024)}, u32[]{:S(2)}) copy-start(f32[2560]{0:T(1024)} %param.23) | copy-start | bytes 30724
  304.2 176.6 %all-reduce.5.cloned.1.call-start = ((), (), s32[]{:S(2)}) async-start(), calls=%async_computation.6 | async-start | bytes 983040 | tf_op jit(solution)/shard_map/psum | solution.py:169
Sparse Core Ops, SparseCore 0:
  14.1 15.5 reduce-scatter.1
  304.3 85.5 all-reduce.2
  397.6 83.0 all-reduce.4
where the time goes:
time: 491 us; the launch traced here: 489 us
  local copies, waits for them, and re-layouts  194 us (40%)
  waiting for transfers between devices  181 us (37%)
  blocking collectives  36.5 us (7%)
  matrix products  27.1 us (6%)
  other arithmetic  22.4 us (5%)
  between operations  14.1 us (3%)
  starting transfers between devices  13.6 us (3%)
    scatter x1, local copies, waits for them, and re-layouts, per_device(): block_all = jnp.zeros((holder_count * slot_count,), jnp.int32).at[target]...  90.5 us
    scatter x1, local copies, waits for them, and re-layouts, per_device(): owner_all = jnp.full((holder_count * slot_count,), -1, jnp.int32).at[targ...  90.2 us
    psum x1, waiting for transfers between devices, per_device(): mixed = lax.psum(partial_out, 'wide')  85.7 us
    psum x1, waiting for transfers between devices, per_device(): lax.psum(down, ('wide', 'narrow'))  83.2 us
    all_gather x1, blocking collectives, per_device(): all_queries = lax.all_gather(query, ('pool', 'narrow'), axis=0, tiled=True)  32 us
  transfers between devices with their start and end apart: 6, of which 4 were waited for; matrix products, arithmetic and copies ran while one was open for 42% of the time, Pallas kernels for 0%

commit v1 on v0

--- a/solution.py
+++ b/solution.py
@@ -68,7 +68,10 @@
     ).astype(jnp.bfloat16)
     key_new = rotate(rms_scale(proj[:, :, group], k_gain), position[:, None]).astype(jnp.bfloat16)
     value_new = proj[:, :, group + 1].astype(jnp.bfloat16)
-    all_queries = lax.all_gather(query, ("pool", "narrow"), axis=0, tiled=True)
+    size = lax.axis_size(("pool", "narrow"))
+    tiles = jnp.stack([query for _ in range(size)])
+    tiles = lax.all_to_all(tiles, ("pool", "narrow"), split_axis=0, concat_axis=0)
+    all_queries = jnp.concatenate(tiles, axis=0)
     slot_count = key_cache.shape[0]
     half_page = key_cache.shape[2]
     holder_count = lax.axis_size("pool")

time: 491 us -> 475 us (0.967)
  blocking collectives: 36.5 us -> 4.5 us
  waiting for transfers between devices: 181 us -> 187 us
  starting transfers between devices: 13.6 us -> 19.4 us
    all_gather x1 -> x0, blocking collectives: 32 us -> none  [per_device(): all_queries = lax.all_gather(query, ('pool', 'narrow'), axis=0, tiled=True)]
    all_to_all x0 -> x1, waiting for transfers between devices: none -> 5.96 us  [per_device(): lax.all_to_all(tiles, ('pool', 'narrow'), split_axis=0, concat_axis=0)]
    all_to_all x0 -> x1, starting transfers between devices: none -> 5.83 us  [per_device(): lax.all_to_all(tiles, ('pool', 'narrow'), split_axis=0, concat_axis=0)]
  transfers between devices with their start and end apart: 6 -> 7, of which waited for: 4 -> 5; matrix products, arithmetic and copies ran while one was open for 42% -> 44% of each run, Pallas kernels for 0% -> 0%
where the time goes in v1:
time: 475 us; the launch traced here: 474 us
  local copies, waits for them, and re-layouts  195 us (41%)
  waiting for transfers between devices  187 us (39%)
  matrix products  27.8 us (6%)
  other arithmetic  24.9 us (5%)
  starting transfers between devices  19.4 us (4%)
  between operations  14 us (3%)
    scatter x1, local copies, waits for them, and re-layouts, per_device(): block_all = jnp.zeros((holder_count * slot_count,), jnp.int32).at[target]...  90.5 us
    scatter x1, local copies, waits for them, and re-layouts, per_device(): owner_all = jnp.full((holder_count * slot_count,), -1, jnp.int32).at[targ...  90.2 us
    psum x1, waiting for transfers between devices, per_device(): mixed = lax.psum(partial_out, 'wide')  85.7 us
    psum x1, waiting for transfers between devices, per_device(): lax.psum(down, ('wide', 'narrow'))  83.2 us
  transfers between devices with their start and end apart: 7, of which 5 were waited for; matrix products, arithmetic and copies ran while one was open for 44% of the time, Pallas kernels for 0%

profile of v1, /device:TPU:0, one launch (start us, length us, event | category | flops | bytes accessed | tf_op | source)
XLA Modules:
  0.0 473.6 jit_solution(7095109864976983266)
XLA Ops:
  7.2 1.2 multiply_reduce_fusion.1
  8.5 1.8 convert_element_type.66
  10.3 0.8 dynamic-slice
  11.0 2.9 fusion.9
  15.7 90.5 %scatter_custom_fusion.1 = s32[2304]{0:T(1024)S(1)} fusion(s32[24576]{0:T(1024)S(1)} %bitcast.106, s32[24576]{0:T(1024)} %fusion.32, s32[]{:T(128)} %constant.29.clone.1), kind=kCustom, calls=%fused_computation.110 | custom fusion | bytes 9728 | tf_op jit(solution)/shard_map/scatter | solution.py:91
  106.1 90.2 %scatter_custom_fusion = s32[2304]{0:T(1024)S(1)} fusion(s32[24576]{0:T(1024)S(1)} %bitcast.107, s32[24576]{0:T(1024)S(1)} %add_select_fusion, s32[]{:T(128)} %constant.28.clone.1), kind=kCustom, calls=%fused_computation.112 | custom fusion | bytes 9220 | tf_op jit(solution)/shard_map/scatter | solution.py:86
  196.6 2.4 gather_fusion
  199.3 0.8 iota_compare_fusion
  200.1 0.8 multiply_reduce_fusion.4
  200.9 0.9 multiply_reduce_fusion.3
  201.8 0.8 multiply_multiply_fusion.1
  202.6 1.4 fusion.77
  204.0 0.9 multiply_multiply_fusion
  204.9 0.8 fusion.59
  206.4 0.8 stack.2
  207.2 5.8 %all-to-all-start = ((bf16[16,24,1,4,128]{4,3,2,1,0:T(4,128)(2,1)}), bf16[16,24,1,4,128]{4,3,2,1,0:T(4,128)(2,1)S(1)}, u32[]{:S(2)}, u32[]{:S(2)}) async-start(bf16[16,24,1,4,128]{4,3,2,1,0:T(4,128)(2,1)} %stack.2), calls=%async_computation.1 | async-start | bytes 786432 | tf_op jit(solution)/shard_map/all_to_all | solution.py:73
  213.1 1.3 fusion.71
  214.4 0.8 maximum_bitcast_fusion
  215.1 1.5 fusion.68
  216.6 6.0 %all-to-all-done = bf16[16,24,1,4,128]{4,3,2,1,0:T(4,128)(2,1)S(1)} async-done(((bf16[16,24,1,4,128]{4,3,2,1,0:T(4,128)(2,1)}), bf16[16,24,1,4,128]{4,3,2,1,0:T(4,128)(2,1)S(1)}, u32[]{:S(2)}, u32[]{:S(2)}) %all-to-all-start) | async-done | bytes 393248 | tf_op jit(solution)/shard_map/all_to_all | solution.py:73
  222.6 2.4 gather_fusion.1
  225.0 5.8 %select_reduce_fusion.1 = (f32[288,4]{1,0:T(8,128)S(1)}, f32[288,4,64]{2,1,0:T(4,128)}) fusion(pred[288,64]{1,0:T(8,128)(4,1)S(1)} %fusion.36, bf16[288,4,128]{2,1,0:T(4,128)(2,1)} %gather_fusion.1, bf16[288,1,64,128]{3,2,1,0:T(8,128)(2,1)} %param.18), kind=kOutput, calls=%fused_computation.23 | convolution fusion | flops 19094400 | bytes 5331456 | tf_op jit(solution)/shard_map/skgd,sktd->skgt/dot_general | solution.py:106
  231.4 0.8 copy.68
  232.2 3.5 all-to-all-start.2
  235.7 1.7 gather_fusion.2
  237.5 1.9 fusion.16
  239.4 4.8 %fusion = f32[288,4,128]{2,1,0:T(4,128)} fusion(bf16[288,1,64,128]{3,2,1,0:T(8,128)(2,1)} %param.19, f32[288,4,64]{2,1,0:T(4,128)} %get-tuple-element.13, f32[288,4]{1,0:T(8,128)} %gather_fusion.2, pred[288,64]{1,0:T(8,128)(4,1)} %copy-done.5), kind=kOutput, calls=%fused_computation.5 | convolution fusion | flops 19095552 | bytes 5626368 | tf_op jit(solution)/shard_map/skgt,sktd->skgd/dot_general | solution.py:114
  244.2 1.4 fusion.29
  245.6 5.6 %all-to-all-start.3 = ((f32[1,384,1,4]{3,2,0,1:T(1,128)}), f32[1,384,1,4]{3,2,0,1:T(1,128)S(1)}, u32[]{:S(2)}, u32[]{:S(2)}) async-start(f32[1,384,1,4]{3,2,0,1:T(1,128)} %bitcast.104), calls=%async_computation.4 | async-start | bytes 393216 | tf_op jit(solution)/shard_map/all_to_all | solution.py:138
  251.3 2.0 convolution_bitcast_fusion
  253.3 1.4 copy.67
  255.3 3.5 all-to-all-done.3
  259.5 4.3 all-to-all-start.1
  263.8 0.8 multiply_maximum_fusion
  265.9 1.7 copy.69
  267.6 1.0 multiply_reduce_fusion.2
  268.6 0.7 convert_convert_fusion
  269.5 8.9 %all-to-all-done.1 = f32[1,384,1,4,128]{4,3,2,0,1:T(4,128)} async-done(((f32[1,384,1,4,128]{4,3,2,0,1:T(4,128)}), f32[1,384,1,4,128]{4,3,2,0,1:T(4,128)}, u32[]{:S(2)}, u32[]{:S(2)}) %all-to-all-start.1) | async-done | bytes 786464 | tf_op jit(solution)/shard_map/all_to_all | solution.py:136
  278.4 1.4 fusion.12
  279.9 0.8 copy_bitcast_fusion
  280.7 4.5 all_gather.3
  285.2 3.1 fusion.82
  288.3 85.7 %all-reduce.3.cloned.1.call-done = f32[48,2560]{1,0:T(8,128)} async-done(((f32[48,2560]{1,0:T(8,128)}), f32[48,2560]{1,0:T(8,128)}) %all-reduce.3.cloned.1.call-update) | async-done | bytes 491536 | tf_op jit(solution)/shard_map/psum | solution.py:166
  374.0 1.2 multiply_reduce_fusion
  375.3 4.9 %fusion.23 = f32[48,2,608]{2,0,1:T(8,128)S(1)} fusion(bf16[2560,2,608]{0,2,1:T(8,128)(2,1)} %param.24, f32[2560]{0:T(1024)S(1)} %copy-done.12, f32[48]{0:T(128)S(1)} %add_rsqrt_fusion.1, f32[48,2560]{1,0:T(8,128)} %all-reduce.3.cloned.1.call-done, bf16[48,2560]{1,0:T(8,128)(2,1)S(1)} %copy-done.2), kind=kOutput, calls=%fused_computation.36 | convolution fusion | flops 299458560 | bytes 7207104 | tf_op jit(solution)/shard_map/rd,dcf->rcf/dot_general | solution.py:29
  380.2 1.4 fusion.50
  381.6 83.2 %all-reduce.5.cloned.1.call-done = f32[48,2560]{1,0:T(8,128)} async-done(((f32[48,2560]{1,0:T(8,128)}), f32[48,2560]{1,0:T(8,128)}) %all-reduce.5.cloned.1.call-update) | async-done | bytes 491536 | tf_op jit(solution)/shard_map/psum | solution.py:172
  464.9 2.2 add_convert_fusion
  (61 shorter events, 6.4 us)
Async XLA Ops:
  7.2 373.0 %copy-start = (bf16[608,2560]{1,0:T(8,128)(2,1)S(1)}, bf16[608,2560]{1,0:T(8,128)(2,1)}, u32[]{:S(2)}) copy-start(bf16[608,2560]{1,0:T(8,128)(2,1)} %param.25) | copy-start | bytes 9338884
  7.2 8.0 %copy-start.8 = (s32[384,64]{0,1:T(8,128)S(1)}, s32[384,64]{0,1:T(8,128)}, u32[]{:S(2)}) copy-start(s32[384,64]{0,1:T(8,128)} %param.21) | copy-start | bytes 294916
  7.2 189.4 %copy-start.1 = (s32[384]{0:T(512)S(1)}, s32[384]{0:T(512)}, u32[]{:S(2)}) copy-start(s32[384]{0:T(512)} %param.20) | copy-start | bytes 4612
  7.2 192.9 %reduce-scatter.2.cloned.1.call-start = ((), (), s32[]{:S(2)}) async-start(), calls=%async_computation.5 | async-start | bytes 221184 | tf_op jit(solution)/shard_map/reduce_scatter | solution.py:60
  10.3 191.6 %copy-start.13 = (f32[128]{0:T(128)S(1)}, f32[128]{0:T(128)}, u32[]{:S(2)}) copy-start(f32[128]{0:T(128)} %param.17) | copy-start | bytes 1540
  196.5 10.8 %copy-start.9 = (s32[288]{0:T(512)}, s32[288]{0:T(512)S(1)}, u32[]{:S(2)}) copy-start(s32[288]{0:T(512)S(1)} %get-tuple-element.3) | copy-start | bytes 3460
  196.5 34.4 %copy-start.11 = (s32[1024]{0:T(1024)}, s32[1024]{0:T(1024)S(1)}, u32[]{:S(2)}) copy-start(s32[1024]{0:T(1024)S(1)} %pad_clamp_fusion) | copy-start | bytes 12292
  199.2 31.7 %copy-start.5 = (pred[288,64]{1,0:T(8,128)(4,1)}, pred[288,64]{1,0:T(8,128)(4,1)S(1)}, u32[]{:S(2)}) copy-start(pred[288,64]{1,0:T(8,128)(4,1)S(1)} %fusion.36) | copy-start | bytes 55300
  205.8 0.6 copy-start.7
  207.2 15.4 %all-to-all-start = ((bf16[16,24,1,4,128]{4,3,2,1,0:T(4,128)(2,1)}), bf16[16,24,1,4,128]{4,3,2,1,0:T(4,128)(2,1)S(1)}, u32[]{:S(2)}, u32[]{:S(2)}) async-start(bf16[16,24,1,4,128]{4,3,2,1,0:T(4,128)(2,1)} %stack.2), calls=%async_computation.1 | async-start | bytes 786432 | tf_op jit(solution)/shard_map/all_to_all | solution.py:73
  225.0 5.9 %copy-start.4 = (pred[288,384]{1,0:T(8,128)(4,1)S(1)}, pred[288,384]{1,0:T(8,128)(4,1)}, u32[]{:S(2)}) copy-start(pred[288,384]{1,0:T(8,128)(4,1)} %iota_compare_fusion) | copy-start | bytes 331780
  232.2 13.4 %all-to-all-start.2 = ((f32[1,384,1,4]{3,2,0,1:T(1,128)}), f32[1,384,1,4]{3,2,0,1:T(1,128)S(1)}, u32[]{:S(2)}, u32[]{:S(2)}) async-start(f32[1,384,1,4]{3,2,0,1:T(1,128)} %copy.68), calls=%async_computation.3 | async-start | bytes 393216 | tf_op jit(solution)/shard_map/all_to_all | solution.py:137
  239.4 4.8 %copy-start.10 = (s32[288]{0:T(512)S(1)}, s32[288]{0:T(512)}, u32[]{:S(2)}) copy-start(s32[288]{0:T(512)} %copy-done.9) | copy-start | bytes 3460
  245.6 13.2 %all-to-all-start.3 = ((f32[1,384,1,4]{3,2,0,1:T(1,128)}), f32[1,384,1,4]{3,2,0,1:T(1,128)S(1)}, u32[]{:S(2)}, u32[]{:S(2)}) async-start(f32[1,384,1,4]{3,2,0,1:T(1,128)} %bitcast.104), calls=%async_computation.4 | async-start | bytes 393216 | tf_op jit(solution)/shard_map/all_to_all | solution.py:138
  258.8 0.7 copy-start.3
  259.5 19.0 %all-to-all-start.1 = ((f32[1,384,1,4,128]{4,3,2,0,1:T(4,128)}), f32[1,384,1,4,128]{4,3,2,0,1:T(4,128)}, u32[]{:S(2)}, u32[]{:S(2)}) async-start(f32[1,384,1,4,128]{4,3,2,0,1:T(4,128)} %copy.67), calls=%async_computation.2 | async-start | bytes 1572864 | tf_op jit(solution)/shard_map/all_to_all | solution.py:136
  263.8 110.3 %copy-start.2 = (bf16[48,2560]{1,0:T(8,128)(2,1)S(1)}, bf16[48,2560]{1,0:T(8,128)(2,1)}, u32[]{:S(2)}) copy-start(bf16[48,2560]{1,0:T(8,128)(2,1)} %param.13) | copy-start | bytes 737284
  263.8 110.3 %all-reduce.3.cloned.1.call-start = ((), (), s32[]{:S(2)}) async-start(), calls=%async_computation.6 | async-start | bytes 983040 | tf_op jit(solution)/shard_map/psum | solution.py:166
  264.6 0.6 copy-start.6
  268.6 106.7 %copy-start.12 = (f32[2560]{0:T(1024)S(1)}, f32[2560]{0:T(1024)}, u32[]{:S(2)}) copy-start(f32[2560]{0:T(1024)} %param.23) | copy-start | bytes 30724
  288.3 176.6 %all-reduce.5.cloned.1.call-start = ((), (), s32[]{:S(2)}) async-start(), calls=%async_computation.7 | async-start | bytes 983040 | tf_op jit(solution)/shard_map/psum | solution.py:172
Sparse Core Ops, SparseCore 0:
  14.1 15.4 reduce-scatter.1
  288.4 85.5 all-reduce.2
  381.8 83.0 all-reduce.4
